TPU v7x, 128 devices: a whole 4x4x4 slice. The times are simulated.
128 devices in a mesh: row: 16 (over y, x), col: 8 (over z, core).
Axes of the slice: x: 4, y: 4, z: 4, core: 2. Of those that a mesh axis runs over, the one named last changes fastest.
Arguments:
- src_points: bfloat16 [16384, 256], P('row'), may hold values from -32 to 32, as said below
- tgt_points: bfloat16 [32768, 256], P(('col', 'row')), may hold values from -32 to 32, as said below
- log_src_mass: float32 [16384], P('row'), may hold values from -3 to 3
- log_tgt_mass: float32 [32768], P('col'), may hold values from -3 to 3
Outputs:
- src_potential: float32 [16384], P('row')
- tgt_potential: float32 [32768], P('col')
- mean_potentials: float32 [], replicated
Inputs may be any that keep to these rules, and one draw needn't show every extreme that they name: `src_points`: point coordinates. `tgt_points`: point coordinates.
All inputs are finite; a program needn't handle non-finite values.
Results may differ from a plain program's by a relative error of at most 0.0003.
Values may be sent and summed in bfloat16 or wider, within the bound.
No kernel may reach another device: no remote copies, remote signals or barrier semaphores. Data moves between devices by JAX's collectives and lax.ppermute only.
A program may use at most 64 MiB of HBM per device.

v0:
```python
import jax
import jax.numpy as jnp
from jax import lax
from jax.sharding import Mesh
from jax.sharding import PartitionSpec as P

ITERS = 3
ROW = ("row_0", "row_1")
COL = ("col_0", "col_1")
ROW_COL = ("row_0", "row_1", "col_0", "col_1")
COL_ROW = ("col_0", "col_1", "row_0", "row_1")
entropy_weight = 0.1


def from_everyone(value, axis):
    peers = lax.axis_size(axis)
    return lax.all_to_all(
        jnp.broadcast_to(value[None], (peers, *value.shape)), axis, 0, 0, tiled=True
    )


def laid_out(tiles, dim):
    shape = list(tiles.shape[1:])
    shape[dim] *= tiles.shape[0]
    return jnp.moveaxis(tiles, 0, dim).reshape(shape)


def gathered_copies(value, axis, dim):
    tiles = from_everyone(value, axis)
    return laid_out(tiles, dim)


def collected_together(value, axis):
    leaves = jax.tree.leaves(value)
    sequence = sorted(range(len(leaves)), key=lambda k: -leaves[k].size)
    width = (1, *leaves[sequence[0]].shape)[-1]
    lines = [
        jnp.pad(leaves[k].reshape(-1), (0, -leaves[k].size % width)).reshape(-1, width)
        for k in sequence
    ]
    both, at, found = (from_everyone(jnp.concatenate(lines), axis), 0, {})
    for k, line in zip(sequence, lines):
        section = both[:, at : at + len(line)].reshape(len(both), -1)
        found[k] = section[:, : leaves[k].size].reshape(-1, *leaves[k].shape)
        at += len(line)
    numbers = iter(range(len(leaves)))
    return jax.tree.map(lambda _: found[next(numbers)], value)


def once_a_type(value, axis):
    leaves, found = (jax.tree.leaves(value), {})
    for leading, a in enumerate(leaves):
        if leading not in found:
            alike = [k for k, b in enumerate(leaves) if b.dtype == a.dtype]
            got = (
                collected_together([leaves[k] for k in alike], axis)
                if len(alike) > 1
                else [from_everyone(a, axis)]
            )
            for k, b in zip(alike, got):
                found[k] = b
    numbers = iter(range(len(leaves)))
    return jax.tree.map(lambda _: found[next(numbers)], value)


def folded_in_pairs(pieces, combine):
    while len(jax.tree.leaves(pieces)[0]) > 1:
        pieces = jax.vmap(combine)(
            *(jax.tree.map(lambda part: part[side::2], pieces) for side in (0, 1))
        )
    return jax.tree.map(lambda part: part[0], pieces)


def combined_all(value, axis, combine):
    pieces = once_a_type(value, axis)
    return folded_in_pairs(pieces, combine)


def joined_all(value, axis, combine):
    pieces = collected_together(value, axis)
    return folded_in_pairs(pieces, combine)


def over_axes(value, axes):
    for axis in axes:
        value = lax.psum(value, axis)
    return value


def cost_block(points_a, squares_a, points_b, squares_b):
    product = lax.dot_general(
        points_a, points_b, (((1,), (1,)), ((), ())), preferred_element_type=jnp.float32
    )
    return (squares_a[:, None] + squares_b[None, :] - 2.0 * product) / points_a.shape[1]


def combine(early, later):
    top = jnp.maximum(early[0], later[0])
    return (top, early[1] * jnp.exp(early[0] - top) + later[1] * jnp.exp(later[0] - top))


def body(src_points, tgt_points, log_src_mass, log_tgt_mass):
    targets = gathered_copies(tgt_points, ROW, 0)
    sqy = jnp.sum(targets.astype(jnp.float32) ** 2, axis=1)
    count = src_points.shape[0]
    block = min(256, count)
    blocks = count // block
    src_blocks = src_points.reshape(blocks, block, -1)
    sq_blocks = jnp.sum(src_points.astype(jnp.float32) ** 2, axis=1).reshape(blocks, block)
    mass_blocks = log_src_mass.reshape(blocks, block)
    width_tgt = targets.shape[0]
    tgt_potential = jnp.zeros((width_tgt,), jnp.float32)
    src_potential = jnp.zeros((count,), jnp.float32)
    for step in range(ITERS):

        def row_terms(points, squares):
            cost = cost_block(points, squares, targets, sqy)
            return log_tgt_mass[None, :] + (tgt_potential[None, :] - cost) / entropy_weight

        def row_pair(item):
            terms = row_terms(item[0], item[1])
            top = jnp.max(terms, axis=1)
            return (top, jnp.sum(jnp.exp(terms - top[:, None]), axis=1))

        top, total = lax.map(row_pair, (src_blocks, sq_blocks))
        top, total = combined_all((top.reshape(-1), total.reshape(-1)), COL, combine)
        src_potential = -entropy_weight * (top + jnp.log(total))
        pot_blocks = src_potential.reshape(blocks, block)

        def col_terms(points, squares, mass, pot):
            cost = cost_block(points, squares, targets, sqy)
            return mass[:, None] + (pot[:, None] - cost) / entropy_weight

        def pair_step(carry, item):
            terms = col_terms(item[0], item[1], item[2], item[3])
            block_top = jnp.max(terms, axis=0)
            block_sum = jnp.sum(jnp.exp(terms - block_top[None, :]), axis=0)
            return (combine(carry, (block_top, block_sum)), None)

        start = (
            jnp.full((width_tgt,), -jnp.inf, jnp.float32),
            jnp.zeros((width_tgt,), jnp.float32),
        )
        inputs = (src_blocks, sq_blocks, mass_blocks, pot_blocks)
        (top, total), unused = lax.scan(pair_step, start, inputs)
        top, total = joined_all((top, total), ROW, combine)
        tgt_potential = -entropy_weight * (top + jnp.log(total))
    sources_all = count * lax.axis_size(ROW)
    targets_all = width_tgt * lax.axis_size(COL)
    local = jnp.sum(src_potential) / (sources_all * lax.axis_size(COL)) + jnp.sum(tgt_potential) / (
        targets_all * lax.axis_size(ROW)
    )
    mean_potentials = over_axes(local, ROW_COL)
    return (src_potential, tgt_potential, mean_potentials)


def solution(mesh):
    finer = Mesh(mesh.devices.reshape(4, 4, 4, 2), ("row_0", "row_1", "col_0", "col_1"))
    placed = (P(ROW, None), P(COL_ROW, None), P(ROW), P(COL))
    return jax.shard_map(
        body, mesh=finer, in_specs=placed, out_specs=(P(ROW), P(COL), P()), check_vma=False
    )
```

profile of v0, /device:TPU:1, one launch (start us, length us, event | category | flops | bytes accessed | tf_op | source)
XLA Modules:
  0.0 220.8 jit_solution(14711009485905905026)
XLA Ops:
  0.7 2.5 %broadcast_in_dim.47 = bf16[16,256,256]{2,1,0:T(8,128)(2,1)} broadcast(bf16[256,256]{1,0:T(8,128)(2,1)} %param.17), dimensions={1,2} | broadcast | bytes 2228224 | tf_op jit(solution)/shard_map/broadcast_in_dim | solution.py:18
  3.2 7.6 %all-to-all-start = ((bf16[16,256,256]{2,1,0:T(8,128)(2,1)}), bf16[16,256,256]{2,1,0:T(8,128)(2,1)S(1)}, u32[]{:S(2)}, u32[]{:S(2)}) async-start(bf16[16,256,256]{2,1,0:T(8,128)(2,1)} %broadcast_in_dim.47), calls=%async_computation | async-start | bytes 4194304 | tf_op jit(solution)/shard_map/all_to_all | solution.py:17
  11.0 30.2 %all-to-all-done = bf16[16,256,256]{2,1,0:T(8,128)(2,1)S(1)} async-done(((bf16[16,256,256]{2,1,0:T(8,128)(2,1)}), bf16[16,256,256]{2,1,0:T(8,128)(2,1)S(1)}, u32[]{:S(2)}, u32[]{:S(2)}) %all-to-all-start) | async-done | bytes 2097184 | tf_op jit(solution)/shard_map/all_to_all | solution.py:17
  41.9 9.3 %while.75 = (s32[]{:T(128)}, f32[4,256]{1,0:T(4,128)S(1)}, f32[4,256]{1,0:T(4,128)S(1)}, f32[4096]{0:T(1024)S(1)}, f32[4,256]{1,0:T(4,128)S(1)}, /*index=5*/f32[...) while((s32[]{:T(128)}, f32[4,256]{1,0:T(4,128)S(1)}, ...), condition=%wide.region_5.6_spmd, body=%wide.region_2.5_spmd.sunk | while | flops 547356160 | bytes 10659957 | solution.py:125
  51.9 7.4 %all-to-all-start.1 = ((f32[8,2,1024]{2,1,0:T(2,128)}), f32[8,2,1024]{2,1,0:T(2,128)S(1)}, u32[]{:S(2)}, u32[]{:S(2)}) async-start(f32[8,2,1024]{2,1,0:T(2,128)} %broadcast_in_dim.48), calls=%async_computation.1 | async-start | bytes 131072 | tf_op jit(solution)/shard_map/all_to_all | solution.py:17
  59.4 4.8 %all-to-all-done.1 = f32[8,2,1024]{2,1,0:T(2,128)S(1)} async-done(((f32[8,2,1024]{2,1,0:T(2,128)}), f32[8,2,1024]{2,1,0:T(2,128)S(1)}, u32[]{:S(2)}, u32[]{:S(2)}) %all-to-all-start.1) | async-done | bytes 65568 | tf_op jit(solution)/shard_map/all_to_all | solution.py:17
  64.6 8.5 %while.78 = (s32[]{:T(128)}, f32[4096]{0:T(1024)S(1)}, f32[4096]{0:T(1024)S(1)}, f32[4,256]{1,0:T(4,128)S(1)}, f32[4,256]{1,0:T(4,128)S(1)}, /*index=5*/f32[4,25...) while((s32[]{:T(128)}, f32[4096]{0:T(1024)S(1)}, ...), condition=%wide.region_9.10_spmd.clone, body=%wide.region_6.9_spmd.clone.sunk | while | flops 547381248 | bytes 10790019 | solution.py:145
  74.1 3.6 %all-to-all-start.2 = ((f32[16,2,4096]{2,1,0:T(2,128)}), f32[16,2,4096]{2,1,0:T(2,128)S(1)}, u32[]{:S(2)}, u32[]{:S(2)}) async-start(f32[16,2,4096]{2,1,0:T(2,128)} %broadcast_in_dim.49), calls=%async_computation.2 | async-start | bytes 1048576 | tf_op jit(solution)/shard_map/all_to_all | solution.py:17
  77.7 10.5 %all-to-all-done.2 = f32[16,2,4096]{2,1,0:T(2,128)S(1)} async-done(((f32[16,2,4096]{2,1,0:T(2,128)}), f32[16,2,4096]{2,1,0:T(2,128)S(1)}, u32[]{:S(2)}, u32[]{:S(2)}) %all-to-all-start.2) | async-done | bytes 524320 | tf_op jit(solution)/shard_map/all_to_all | solution.py:17
  90.8 9.4 %while.76 = (s32[]{:T(128)}, f32[4,256]{1,0:T(4,128)S(1)}, f32[4,256]{1,0:T(4,128)S(1)}, f32[4096]{0:T(1024)S(1)}, f32[4096]{0:T(1024)S(1)}, /*index=5*/f32[4,25...) while((s32[]{:T(128)}, f32[4,256]{1,0:T(4,128)S(1)}, ...), condition=%wide.region_13.14_spmd, body=%wide.region_10.13_spmd.sunk | while | flops 547356160 | bytes 10676349 | solution.py:125
  90.8 1.5 fusion.101
  93.2 1.5 fusion.101
  95.5 1.5 fusion.101
  100.8 5.2 %all-to-all-start.3 = ((f32[8,2,1024]{2,1,0:T(2,128)}), f32[8,2,1024]{2,1,0:T(2,128)S(1)}, u32[]{:S(2)}, u32[]{:S(2)}) async-start(f32[8,2,1024]{2,1,0:T(2,128)} %broadcast_in_dim.50), calls=%async_computation.3 | async-start | bytes 131072 | tf_op jit(solution)/shard_map/all_to_all | solution.py:17
  106.0 4.9 %all-to-all-done.3 = f32[8,2,1024]{2,1,0:T(2,128)S(1)} async-done(((f32[8,2,1024]{2,1,0:T(2,128)}), f32[8,2,1024]{2,1,0:T(2,128)S(1)}, u32[]{:S(2)}, u32[]{:S(2)}) %all-to-all-start.3) | async-done | bytes 65568 | tf_op jit(solution)/shard_map/all_to_all | solution.py:17
  111.3 8.5 %while.79 = (s32[]{:T(128)}, f32[4096]{0:T(1024)S(1)}, f32[4096]{0:T(1024)S(1)}, f32[4,256]{1,0:T(4,128)S(1)}, f32[4,256]{1,0:T(4,128)S(1)}, /*index=5*/f32[4,25...) while((s32[]{:T(128)}, f32[4096]{0:T(1024)S(1)}, ...), condition=%wide.region_17.18_spmd.clone, body=%wide.region_14.17_spmd.clone.sunk | while | flops 547381248 | bytes 10790019 | solution.py:145
  120.8 3.6 %all-to-all-start.4 = ((f32[16,2,4096]{2,1,0:T(2,128)}), f32[16,2,4096]{2,1,0:T(2,128)S(1)}, u32[]{:S(2)}, u32[]{:S(2)}) async-start(f32[16,2,4096]{2,1,0:T(2,128)} %broadcast_in_dim.56), calls=%async_computation.4 | async-start | bytes 1048576 | tf_op jit(solution)/shard_map/all_to_all | solution.py:17
  124.4 10.5 %all-to-all-done.4 = f32[16,2,4096]{2,1,0:T(2,128)S(1)} async-done(((f32[16,2,4096]{2,1,0:T(2,128)}), f32[16,2,4096]{2,1,0:T(2,128)S(1)}, u32[]{:S(2)}, u32[]{:S(2)}) %all-to-all-start.4) | async-done | bytes 524320 | tf_op jit(solution)/shard_map/all_to_all | solution.py:17
  137.5 9.4 %while.77 = (s32[]{:T(128)}, f32[4,256]{1,0:T(4,128)S(1)}, f32[4,256]{1,0:T(4,128)S(1)}, f32[4096]{0:T(1024)S(1)}, f32[4096]{0:T(1024)S(1)}, /*index=5*/f32[4,25...) while((s32[]{:T(128)}, f32[4,256]{1,0:T(4,128)S(1)}, ...), condition=%wide.region_21.22_spmd, body=%wide.region_18.21_spmd.sunk | while | flops 547356160 | bytes 10676349 | solution.py:125
  139.9 1.5 fusion.103
  142.2 1.5 fusion.103
  144.6 1.5 fusion.103
  147.6 5.2 %all-to-all-start.5 = ((f32[8,2,1024]{2,1,0:T(2,128)}), f32[8,2,1024]{2,1,0:T(2,128)S(1)}, u32[]{:S(2)}, u32[]{:S(2)}) async-start(f32[8,2,1024]{2,1,0:T(2,128)} %broadcast_in_dim.57), calls=%async_computation.5 | async-start | bytes 131072 | tf_op jit(solution)/shard_map/all_to_all | solution.py:17
  152.7 4.9 %all-to-all-done.5 = f32[8,2,1024]{2,1,0:T(2,128)S(1)} async-done(((f32[8,2,1024]{2,1,0:T(2,128)}), f32[8,2,1024]{2,1,0:T(2,128)S(1)}, u32[]{:S(2)}, u32[]{:S(2)}) %all-to-all-start.5) | async-done | bytes 65568 | tf_op jit(solution)/shard_map/all_to_all | solution.py:17
  158.5 1.9 fusion.63
  160.3 8.4 %while.80 = (s32[]{:T(128)}, f32[4096]{0:T(1024)S(1)}, f32[4096]{0:T(1024)S(1)}, f32[4,256]{1,0:T(4,128)S(1)}, f32[4,256]{1,0:T(4,128)S(1)}, /*index=5*/f32[4,25...) while((s32[]{:T(128)}, f32[4096]{0:T(1024)S(1)}, ...), condition=%wide.region_25.26_spmd.clone, body=%wide.region_22.25_spmd.clone.sunk | while | flops 547381248 | bytes 10790019 | solution.py:145
  169.8 3.6 %all-to-all-start.6 = ((f32[16,2,4096]{2,1,0:T(2,128)}), f32[16,2,4096]{2,1,0:T(2,128)S(1)}, u32[]{:S(2)}, u32[]{:S(2)}) async-start(f32[16,2,4096]{2,1,0:T(2,128)} %broadcast_in_dim.58), calls=%async_computation.6 | async-start | bytes 1048576 | tf_op jit(solution)/shard_map/all_to_all | solution.py:17
  174.0 9.9 %all-to-all-done.6 = f32[16,2,4096]{2,1,0:T(2,128)S(1)} async-done(((f32[16,2,4096]{2,1,0:T(2,128)}), f32[16,2,4096]{2,1,0:T(2,128)S(1)}, u32[]{:S(2)}, u32[]{:S(2)}) %all-to-all-start.6) | async-done | bytes 524320 | tf_op jit(solution)/shard_map/all_to_all | solution.py:17
  188.3 7.2 %psum.28 = f32[]{:T(128)} all-reduce(f32[]{:T(128)S(6)} %add.300), channel_id=1, replica_groups=mesh['row_0'=4,'row_1'=4,'col_0'=4,'col_1'=2] {'row_0'}, use_global_device_ids=true, to_apply=%region_28.29 | all-reduce | flops 1 | bytes 8 | tf_op jit(solution)/shard_map/psum | solution.py:86
  195.5 7.4 %psum.29 = f32[]{:T(128)} all-reduce(f32[]{:T(128)} %psum.28), channel_id=1, replica_groups=mesh['row_0'=4,'row_1'=4,'col_0'=4,'col_1'=2] {'row_1'}, use_global_device_ids=true, to_apply=%region_29.30 | all-reduce | flops 1 | bytes 8 | tf_op jit(solution)/shard_map/psum | solution.py:86
  202.9 7.5 %psum.30 = f32[]{:T(128)} all-reduce(f32[]{:T(128)} %psum.29), channel_id=1, replica_groups=mesh['row_0'=4,'row_1'=4,'col_0'=4,'col_1'=2] {'col_0'}, use_global_device_ids=true, to_apply=%region_30.31 | all-reduce | flops 1 | bytes 8 | tf_op jit(solution)/shard_map/psum | solution.py:86
  210.4 10.4 %psum.31 = f32[]{:T(128)} all-reduce(f32[]{:T(128)} %psum.30), channel_id=1, replica_groups=mesh['row_0'=4,'row_1'=4,'col_0'=4,'col_1'=2] {'col_1'}, use_global_device_ids=true, to_apply=%region_31.32 | all-reduce | flops 1 | bytes 8 | tf_op jit(solution)/shard_map/psum | solution.py:86
  (256 shorter events, 59.4 us)
Async XLA Ops:
  0.6 10.1 %copy-start = (bf16[1024,256]{1,0:T(8,128)(2,1)S(1)}, bf16[1024,256]{1,0:T(8,128)(2,1)}, u32[]{:S(2)}) copy-start(bf16[1024,256]{1,0:T(8,128)(2,1)} %param.16) | copy-start | bytes 1572868
  0.6 41.3 %copy-start.2 = (f32[4096]{0:T(1024)S(1)}, f32[4096]{0:T(1024)}, u32[]{:S(2)}) copy-start(f32[4096]{0:T(1024)} %param.19) | copy-start | bytes 49156
  3.2 38.1 %all-to-all-start = ((bf16[16,256,256]{2,1,0:T(8,128)(2,1)}), bf16[16,256,256]{2,1,0:T(8,128)(2,1)S(1)}, u32[]{:S(2)}, u32[]{:S(2)}) async-start(bf16[16,256,256]{2,1,0:T(8,128)(2,1)} %broadcast_in_dim.47), calls=%async_computation | async-start | bytes 4194304 | tf_op jit(solution)/shard_map/all_to_all | solution.py:17
  41.9 17.4 %copy-start.1 = (f32[1024]{0:T(1024)S(1)}, f32[1024]{0:T(1024)}, u32[]{:S(2)}) copy-start(f32[1024]{0:T(1024)} %param.18) | copy-start | bytes 12292
  51.9 12.3 %all-to-all-start.1 = ((f32[8,2,1024]{2,1,0:T(2,128)}), f32[8,2,1024]{2,1,0:T(2,128)S(1)}, u32[]{:S(2)}, u32[]{:S(2)}) async-start(f32[8,2,1024]{2,1,0:T(2,128)} %broadcast_in_dim.48), calls=%async_computation.1 | async-start | bytes 131072 | tf_op jit(solution)/shard_map/all_to_all | solution.py:17
  74.1 14.1 %all-to-all-start.2 = ((f32[16,2,4096]{2,1,0:T(2,128)}), f32[16,2,4096]{2,1,0:T(2,128)S(1)}, u32[]{:S(2)}, u32[]{:S(2)}) async-start(f32[16,2,4096]{2,1,0:T(2,128)} %broadcast_in_dim.49), calls=%async_computation.2 | async-start | bytes 1048576 | tf_op jit(solution)/shard_map/all_to_all | solution.py:17
  100.8 10.1 %all-to-all-start.3 = ((f32[8,2,1024]{2,1,0:T(2,128)}), f32[8,2,1024]{2,1,0:T(2,128)S(1)}, u32[]{:S(2)}, u32[]{:S(2)}) async-start(f32[8,2,1024]{2,1,0:T(2,128)} %broadcast_in_dim.50), calls=%async_computation.3 | async-start | bytes 131072 | tf_op jit(solution)/shard_map/all_to_all | solution.py:17
  120.8 14.1 %all-to-all-start.4 = ((f32[16,2,4096]{2,1,0:T(2,128)}), f32[16,2,4096]{2,1,0:T(2,128)S(1)}, u32[]{:S(2)}, u32[]{:S(2)}) async-start(f32[16,2,4096]{2,1,0:T(2,128)} %broadcast_in_dim.56), calls=%async_computation.4 | async-start | bytes 1048576 | tf_op jit(solution)/shard_map/all_to_all | solution.py:17
  147.6 10.0 %all-to-all-start.5 = ((f32[8,2,1024]{2,1,0:T(2,128)}), f32[8,2,1024]{2,1,0:T(2,128)S(1)}, u32[]{:S(2)}, u32[]{:S(2)}) async-start(f32[8,2,1024]{2,1,0:T(2,128)} %broadcast_in_dim.57), calls=%async_computation.5 | async-start | bytes 131072 | tf_op jit(solution)/shard_map/all_to_all | solution.py:17
  169.8 14.1 %all-to-all-start.6 = ((f32[16,2,4096]{2,1,0:T(2,128)}), f32[16,2,4096]{2,1,0:T(2,128)S(1)}, u32[]{:S(2)}, u32[]{:S(2)}) async-start(f32[16,2,4096]{2,1,0:T(2,128)} %broadcast_in_dim.58), calls=%async_computation.6 | async-start | bytes 1048576 | tf_op jit(solution)/shard_map/all_to_all | solution.py:17
where the time goes:
time: 222 us; the launch traced here: 221 us
  waiting for transfers between devices  75.8 us (34%)
  starting transfers between devices  36.1 us (16%)
  matrix products  35.4 us (16%)
  blocking collectives  32.4 us (15%)
  other arithmetic  21 us (9%)
  local copies, waits for them, and re-layouts  16.5 us (7%)
  between operations  2.76 us (1%)
    all_to_all x7, waiting for transfers between devices, from_everyone(): lax.all_to_all(jnp.broadcast_to(value[None], (peers, *value.shape)), axis...  75.8 us
    all_to_all x7, starting transfers between devices, from_everyone(): lax.all_to_all(jnp.broadcast_to(value[None], (peers, *value.shape)), axis...  36.1 us
    dot_general x24, matrix products, cost_block(): lax.dot_general(points_a, points_b, (((1,), (1,)), ((), ())), preferred_e...  35.4 us
    psum x4, blocking collectives, over_axes(): value = lax.psum(value, axis)  32.4 us
    reduce_sum x12, other arithmetic, row_pair(): return (top, jnp.sum(jnp.exp(terms - top[:, None]), axis=1))  8.61 us
    broadcast_in_dim x7, local copies, waits for them, and re-layouts, from_everyone(): jnp.broadcast_to(value[None], (peers, *value.shape))  7.4 us
    reduce_sum x12, other arithmetic, pair_step(): block_sum = jnp.sum(jnp.exp(terms - block_top[None, :]), axis=0)  7.15 us
  transfers between devices with their start and end apart: 7, of which 7 were waited for; matrix products, arithmetic and copies ran while one was open for 0% of the time, Pallas kernels for 0%

commit v1 on v0

--- a/solution.py
+++ b/solution.py
@@ -83,7 +83,7 @@
 
 def over_axes(value, axes):
     for axis in axes:
-        value = lax.psum(value, axis)
+        value = jnp.sum(lax.all_gather(value, axis), axis=0)
     return value
 
 

time: 222 us -> 229 us (1.032)
  local copies, waits for them, and re-layouts: 16.5 us -> 24.3 us
  other arithmetic: 21 us -> 23.4 us
  blocking collectives: 32.4 us -> 30 us
    psum x4 -> x0, blocking collectives: 32.4 us -> none  [over_axes(): value = lax.psum(value, axis)]
    unnamed x0 -> x4, blocking collectives: none -> 30 us
    unnamed x23 -> x43, local copies, waits for them, and re-layouts: 1.04 us -> 8.85 us
    reduce_sum x0 -> x4, other arithmetic: none -> 2.41 us  [over_axes(): value = jnp.sum(lax.all_gather(value, axis), axis=0)]
where the time goes in v1:
time: 229 us; the launch traced here: 228 us
  waiting for transfers between devices  75.1 us (33%)
  starting transfers between devices  36.1 us (16%)
  matrix products  35.4 us (15%)
  blocking collectives  30 us (13%)
  local copies, waits for them, and re-layouts  24.3 us (11%)
  other arithmetic  23.4 us (10%)
  between operations  2.82 us (1%)
    all_to_all x7, waiting for transfers between devices, from_everyone(): lax.all_to_all(jnp.broadcast_to(value[None], (peers, *value.shape)), axis...  75.1 us
    all_to_all x7, starting transfers between devices, from_everyone(): lax.all_to_all(jnp.broadcast_to(value[None], (peers, *value.shape)), axis...  36.1 us
    dot_general x24, matrix products, cost_block(): lax.dot_general(points_a, points_b, (((1,), (1,)), ((), ())), preferred_e...  35.4 us
    unnamed x4, blocking collectives  30 us
    unnamed x43, local copies, waits for them, and re-layouts  8.85 us
    reduce_sum x12, other arithmetic, row_pair(): return (top, jnp.sum(jnp.exp(terms - top[:, None]), axis=1))  8.61 us
    broadcast_in_dim x7, local copies, waits for them, and re-layouts, from_everyone(): jnp.broadcast_to(value[None], (peers, *value.shape))  7.4 us
    reduce_sum x12, other arithmetic, pair_step(): block_sum = jnp.sum(jnp.exp(terms - block_top[None, :]), axis=0)  7.15 us
  transfers between devices with their start and end apart: 7, of which 7 were waited for; matrix products, arithmetic and copies ran while one was open for 0% of the time, Pallas kernels for 0%

profile of v1, /device:TPU:1, one launch (start us, length us, event | category | flops | bytes accessed | tf_op | source)
XLA Modules:
  0.0 227.9 jit_solution(1655684943578808172)
XLA Ops:
  0.7 2.5 %broadcast_in_dim.47 = bf16[16,256,256]{2,1,0:T(8,128)(2,1)} broadcast(bf16[256,256]{1,0:T(8,128)(2,1)} %param.17), dimensions={1,2} | broadcast | bytes 2228224 | tf_op jit(solution)/shard_map/broadcast_in_dim | solution.py:18
  3.2 7.6 %all-to-all-start = ((bf16[16,256,256]{2,1,0:T(8,128)(2,1)}), bf16[16,256,256]{2,1,0:T(8,128)(2,1)S(1)}, u32[]{:S(2)}, u32[]{:S(2)}) async-start(bf16[16,256,256]{2,1,0:T(8,128)(2,1)} %broadcast_in_dim.47), calls=%async_computation | async-start | bytes 4194304 | tf_op jit(solution)/shard_map/all_to_all | solution.py:17
  11.0 30.2 %all-to-all-done = bf16[16,256,256]{2,1,0:T(8,128)(2,1)S(1)} async-done(((bf16[16,256,256]{2,1,0:T(8,128)(2,1)}), bf16[16,256,256]{2,1,0:T(8,128)(2,1)S(1)}, u32[]{:S(2)}, u32[]{:S(2)}) %all-to-all-start) | async-done | bytes 2097184 | tf_op jit(solution)/shard_map/all_to_all | solution.py:17
  41.9 9.3 %while.75 = (s32[]{:T(128)}, f32[4,256]{1,0:T(4,128)S(1)}, f32[4,256]{1,0:T(4,128)S(1)}, f32[4096]{0:T(1024)S(1)}, f32[4,256]{1,0:T(4,128)S(1)}, /*index=5*/f32[...) while((s32[]{:T(128)}, f32[4,256]{1,0:T(4,128)S(1)}, ...), condition=%wide.region_5.6_spmd, body=%wide.region_2.5_spmd.sunk | while | flops 547356160 | bytes 10659957 | solution.py:125
  51.9 7.4 %all-to-all-start.1 = ((f32[8,2,1024]{2,1,0:T(2,128)}), f32[8,2,1024]{2,1,0:T(2,128)S(1)}, u32[]{:S(2)}, u32[]{:S(2)}) async-start(f32[8,2,1024]{2,1,0:T(2,128)} %broadcast_in_dim.48), calls=%async_computation.1 | async-start | bytes 131072 | tf_op jit(solution)/shard_map/all_to_all | solution.py:17
  59.4 4.8 %all-to-all-done.1 = f32[8,2,1024]{2,1,0:T(2,128)S(1)} async-done(((f32[8,2,1024]{2,1,0:T(2,128)}), f32[8,2,1024]{2,1,0:T(2,128)S(1)}, u32[]{:S(2)}, u32[]{:S(2)}) %all-to-all-start.1) | async-done | bytes 65568 | tf_op jit(solution)/shard_map/all_to_all | solution.py:17
  64.6 8.5 %while.78 = (s32[]{:T(128)}, f32[4096]{0:T(1024)S(1)}, f32[4096]{0:T(1024)S(1)}, f32[4,256]{1,0:T(4,128)S(1)}, f32[4,256]{1,0:T(4,128)S(1)}, /*index=5*/f32[4,25...) while((s32[]{:T(128)}, f32[4096]{0:T(1024)S(1)}, ...), condition=%wide.region_9.10_spmd.clone, body=%wide.region_6.9_spmd.clone.sunk | while | flops 547381248 | bytes 10790019 | solution.py:145
  74.1 3.6 %all-to-all-start.2 = ((f32[16,2,4096]{2,1,0:T(2,128)}), f32[16,2,4096]{2,1,0:T(2,128)S(1)}, u32[]{:S(2)}, u32[]{:S(2)}) async-start(f32[16,2,4096]{2,1,0:T(2,128)} %broadcast_in_dim.49), calls=%async_computation.2 | async-start | bytes 1048576 | tf_op jit(solution)/shard_map/all_to_all | solution.py:17
  77.7 10.5 %all-to-all-done.2 = f32[16,2,4096]{2,1,0:T(2,128)S(1)} async-done(((f32[16,2,4096]{2,1,0:T(2,128)}), f32[16,2,4096]{2,1,0:T(2,128)S(1)}, u32[]{:S(2)}, u32[]{:S(2)}) %all-to-all-start.2) | async-done | bytes 524320 | tf_op jit(solution)/shard_map/all_to_all | solution.py:17
  90.8 9.4 %while.76 = (s32[]{:T(128)}, f32[4,256]{1,0:T(4,128)S(1)}, f32[4,256]{1,0:T(4,128)S(1)}, f32[4096]{0:T(1024)S(1)}, f32[4096]{0:T(1024)S(1)}, /*index=5*/f32[4,25...) while((s32[]{:T(128)}, f32[4,256]{1,0:T(4,128)S(1)}, ...), condition=%wide.region_13.14_spmd, body=%wide.region_10.13_spmd.sunk | while | flops 547356160 | bytes 10676349 | solution.py:125
  90.8 1.5 fusion.101
  93.2 1.5 fusion.101
  95.5 1.5 fusion.101
  100.8 5.2 %all-to-all-start.3 = ((f32[8,2,1024]{2,1,0:T(2,128)}), f32[8,2,1024]{2,1,0:T(2,128)S(1)}, u32[]{:S(2)}, u32[]{:S(2)}) async-start(f32[8,2,1024]{2,1,0:T(2,128)} %broadcast_in_dim.50), calls=%async_computation.3 | async-start | bytes 131072 | tf_op jit(solution)/shard_map/all_to_all | solution.py:17
  106.0 4.9 %all-to-all-done.3 = f32[8,2,1024]{2,1,0:T(2,128)S(1)} async-done(((f32[8,2,1024]{2,1,0:T(2,128)}), f32[8,2,1024]{2,1,0:T(2,128)S(1)}, u32[]{:S(2)}, u32[]{:S(2)}) %all-to-all-start.3) | async-done | bytes 65568 | tf_op jit(solution)/shard_map/all_to_all | solution.py:17
  111.3 8.5 %while.79 = (s32[]{:T(128)}, f32[4096]{0:T(1024)S(1)}, f32[4096]{0:T(1024)S(1)}, f32[4,256]{1,0:T(4,128)S(1)}, f32[4,256]{1,0:T(4,128)S(1)}, /*index=5*/f32[4,25...) while((s32[]{:T(128)}, f32[4096]{0:T(1024)S(1)}, ...), condition=%wide.region_17.18_spmd.clone, body=%wide.region_14.17_spmd.clone.sunk | while | flops 547381248 | bytes 10790019 | solution.py:145
  120.8 3.6 %all-to-all-start.4 = ((f32[16,2,4096]{2,1,0:T(2,128)}), f32[16,2,4096]{2,1,0:T(2,128)S(1)}, u32[]{:S(2)}, u32[]{:S(2)}) async-start(f32[16,2,4096]{2,1,0:T(2,128)} %broadcast_in_dim.56), calls=%async_computation.4 | async-start | bytes 1048576 | tf_op jit(solution)/shard_map/all_to_all | solution.py:17
  124.4 10.5 %all-to-all-done.4 = f32[16,2,4096]{2,1,0:T(2,128)S(1)} async-done(((f32[16,2,4096]{2,1,0:T(2,128)}), f32[16,2,4096]{2,1,0:T(2,128)S(1)}, u32[]{:S(2)}, u32[]{:S(2)}) %all-to-all-start.4) | async-done | bytes 524320 | tf_op jit(solution)/shard_map/all_to_all | solution.py:17
  137.5 9.4 %while.77 = (s32[]{:T(128)}, f32[4,256]{1,0:T(4,128)S(1)}, f32[4,256]{1,0:T(4,128)S(1)}, f32[4096]{0:T(1024)S(1)}, f32[4096]{0:T(1024)S(1)}, /*index=5*/f32[4,25...) while((s32[]{:T(128)}, f32[4,256]{1,0:T(4,128)S(1)}, ...), condition=%wide.region_21.22_spmd, body=%wide.region_18.21_spmd.sunk | while | flops 547356160 | bytes 10676349 | solution.py:125
  139.9 1.5 fusion.103
  142.2 1.5 fusion.103
  144.6 1.5 fusion.103
  147.6 5.2 %all-to-all-start.5 = ((f32[8,2,1024]{2,1,0:T(2,128)}), f32[8,2,1024]{2,1,0:T(2,128)S(1)}, u32[]{:S(2)}, u32[]{:S(2)}) async-start(f32[8,2,1024]{2,1,0:T(2,128)} %broadcast_in_dim.57), calls=%async_computation.5 | async-start | bytes 131072 | tf_op jit(solution)/shard_map/all_to_all | solution.py:17
  152.7 4.9 %all-to-all-done.5 = f32[8,2,1024]{2,1,0:T(2,128)S(1)} async-done(((f32[8,2,1024]{2,1,0:T(2,128)}), f32[8,2,1024]{2,1,0:T(2,128)S(1)}, u32[]{:S(2)}, u32[]{:S(2)}) %all-to-all-start.5) | async-done | bytes 65568 | tf_op jit(solution)/shard_map/all_to_all | solution.py:17
  158.5 1.9 fusion.63
  160.3 8.5 %while.80 = (s32[]{:T(128)}, f32[4096]{0:T(1024)S(1)}, f32[4096]{0:T(1024)S(1)}, f32[4,256]{1,0:T(4,128)S(1)}, f32[4,256]{1,0:T(4,128)S(1)}, /*index=5*/f32[4,25...) while((s32[]{:T(128)}, f32[4096]{0:T(1024)S(1)}, ...), condition=%wide.region_25.26_spmd.clone, body=%wide.region_22.25_spmd.clone.sunk | while | flops 547381248 | bytes 10790019 | solution.py:145
  169.9 3.6 %all-to-all-start.6 = ((f32[16,2,4096]{2,1,0:T(2,128)}), f32[16,2,4096]{2,1,0:T(2,128)S(1)}, u32[]{:S(2)}, u32[]{:S(2)}) async-start(f32[16,2,4096]{2,1,0:T(2,128)} %broadcast_in_dim.58), calls=%async_computation.6 | async-start | bytes 1048576 | tf_op jit(solution)/shard_map/all_to_all | solution.py:17
  174.8 9.2 %all-to-all-done.6 = f32[16,2,4096]{2,1,0:T(2,128)S(1)} async-done(((f32[16,2,4096]{2,1,0:T(2,128)}), f32[16,2,4096]{2,1,0:T(2,128)S(1)}, u32[]{:S(2)}, u32[]{:S(2)}) %all-to-all-start.6) | async-done | bytes 524320 | tf_op jit(solution)/shard_map/all_to_all | solution.py:17
  189.9 6.7 %all-reduce = f32[4]{0:T(128)S(1)} all-reduce(f32[4]{0:T(128)S(1)} %dynamic-update-slice), channel_id=1, replica_groups=mesh['row_0'=4,'row_1'=4,'col_0'=4,'col_1'=2] {'row_0'}, use_global_device_ids=true, to_apply=%add | all-reduce | flops 4 | bytes 32
  199.2 6.7 %all-reduce.1 = f32[4]{0:T(128)S(1)} all-reduce(f32[4]{0:T(128)S(1)} %dynamic-update-slice.1), channel_id=1, replica_groups=mesh['row_0'=4,'row_1'=4,'col_0'=4,'col_1'=2] {'row_1'}, use_global_device_ids=true, to_apply=%add.1 | all-reduce | flops 4 | bytes 32
  208.7 6.8 %all-reduce.2 = f32[4]{0:T(128)S(1)} all-reduce(f32[4]{0:T(128)S(1)} %dynamic-update-slice.2), channel_id=1, replica_groups=mesh['row_0'=4,'row_1'=4,'col_0'=4,'col_1'=2] {'col_0'}, use_global_device_ids=true, to_apply=%add.2 | all-reduce | flops 4 | bytes 32
  217.6 9.8 %all-reduce.3 = f32[2]{0:T(128)S(1)} all-reduce(f32[2]{0:T(128)S(1)} %dynamic-update-slice.3), channel_id=1, replica_groups=mesh['row_0'=4,'row_1'=4,'col_0'=4,'col_1'=2] {'col_1'}, use_global_device_ids=true, to_apply=%add.3 | all-reduce | flops 2 | bytes 16
  (280 shorter events, 69.6 us)
Async XLA Ops:
  0.6 10.1 %copy-start = (bf16[1024,256]{1,0:T(8,128)(2,1)S(1)}, bf16[1024,256]{1,0:T(8,128)(2,1)}, u32[]{:S(2)}) copy-start(bf16[1024,256]{1,0:T(8,128)(2,1)} %param.16) | copy-start | bytes 1572868
  0.6 41.3 %copy-start.2 = (f32[4096]{0:T(1024)S(1)}, f32[4096]{0:T(1024)}, u32[]{:S(2)}) copy-start(f32[4096]{0:T(1024)} %param.19) | copy-start | bytes 49156
  3.2 38.1 %all-to-all-start = ((bf16[16,256,256]{2,1,0:T(8,128)(2,1)}), bf16[16,256,256]{2,1,0:T(8,128)(2,1)S(1)}, u32[]{:S(2)}, u32[]{:S(2)}) async-start(bf16[16,256,256]{2,1,0:T(8,128)(2,1)} %broadcast_in_dim.47), calls=%async_computation | async-start | bytes 4194304 | tf_op jit(solution)/shard_map/all_to_all | solution.py:17
  41.9 17.4 %copy-start.1 = (f32[1024]{0:T(1024)S(1)}, f32[1024]{0:T(1024)}, u32[]{:S(2)}) copy-start(f32[1024]{0:T(1024)} %param.18) | copy-start | bytes 12292
  51.9 12.3 %all-to-all-start.1 = ((f32[8,2,1024]{2,1,0:T(2,128)}), f32[8,2,1024]{2,1,0:T(2,128)S(1)}, u32[]{:S(2)}, u32[]{:S(2)}) async-start(f32[8,2,1024]{2,1,0:T(2,128)} %broadcast_in_dim.48), calls=%async_computation.1 | async-start | bytes 131072 | tf_op jit(solution)/shard_map/all_to_all | solution.py:17
  74.1 14.1 %all-to-all-start.2 = ((f32[16,2,4096]{2,1,0:T(2,128)}), f32[16,2,4096]{2,1,0:T(2,128)S(1)}, u32[]{:S(2)}, u32[]{:S(2)}) async-start(f32[16,2,4096]{2,1,0:T(2,128)} %broadcast_in_dim.49), calls=%async_computation.2 | async-start | bytes 1048576 | tf_op jit(solution)/shard_map/all_to_all | solution.py:17
  100.8 10.1 %all-to-all-start.3 = ((f32[8,2,1024]{2,1,0:T(2,128)}), f32[8,2,1024]{2,1,0:T(2,128)S(1)}, u32[]{:S(2)}, u32[]{:S(2)}) async-start(f32[8,2,1024]{2,1,0:T(2,128)} %broadcast_in_dim.50), calls=%async_computation.3 | async-start | bytes 131072 | tf_op jit(solution)/shard_map/all_to_all | solution.py:17
  120.8 14.1 %all-to-all-start.4 = ((f32[16,2,4096]{2,1,0:T(2,128)}), f32[16,2,4096]{2,1,0:T(2,128)S(1)}, u32[]{:S(2)}, u32[]{:S(2)}) async-start(f32[16,2,4096]{2,1,0:T(2,128)} %broadcast_in_dim.56), calls=%async_computation.4 | async-start | bytes 1048576 | tf_op jit(solution)/shard_map/all_to_all | solution.py:17
  147.6 10.0 %all-to-all-start.5 = ((f32[8,2,1024]{2,1,0:T(2,128)}), f32[8,2,1024]{2,1,0:T(2,128)S(1)}, u32[]{:S(2)}, u32[]{:S(2)}) async-start(f32[8,2,1024]{2,1,0:T(2,128)} %broadcast_in_dim.57), calls=%async_computation.5 | async-start | bytes 131072 | tf_op jit(solution)/shard_map/all_to_all | solution.py:17
  160.3 13.1 %copy-start.6 = (u32[128]{0:T(128)S(1)}, u32[128]{0:T(128)}, u32[]{:S(2)}) copy-start(u32[128]{0:T(128)} %constant.149) | copy-start | bytes 1540
  168.8 20.4 %copy-start.5 = (u32[128]{0:T(128)S(1)}, u32[128]{0:T(128)}, u32[]{:S(2)}) copy-start(u32[128]{0:T(128)} %constant.154) | copy-start | bytes 1540
  168.8 29.8 %copy-start.4 = (u32[128]{0:T(128)S(1)}, u32[128]{0:T(128)}, u32[]{:S(2)}) copy-start(u32[128]{0:T(128)} %constant.159) | copy-start | bytes 1540
  168.8 39.2 %copy-start.3 = (u32[128]{0:T(128)S(1)}, u32[128]{0:T(128)}, u32[]{:S(2)}) copy-start(u32[128]{0:T(128)} %constant.164) | copy-start | bytes 1540
  169.9 14.1 %all-to-all-start.6 = ((f32[16,2,4096]{2,1,0:T(2,128)}), f32[16,2,4096]{2,1,0:T(2,128)S(1)}, u32[]{:S(2)}, u32[]{:S(2)}) async-start(f32[16,2,4096]{2,1,0:T(2,128)} %broadcast_in_dim.58), calls=%async_computation.6 | async-start | bytes 1048576 | tf_op jit(solution)/shard_map/all_to_all | solution.py:17
